TPU v7x, 32 devices: a whole 2x2x4 slice. The times are simulated.
32 devices in a mesh: src: 8 (over z, y), snk: 4 (over x, core).
Axes of the slice: x: 2, y: 2, z: 4, core: 2. Of those that a mesh axis runs over, the one named last changes fastest.
Arguments:
- tau_cols: bfloat16 [2, 8, 8, 256, 256], P(None, 'src', None, 'snk'), may hold values from -0.25 to 0.25
- elementals: bfloat16 [256, 2, 256, 256], P('src'), may hold values from -0.25 to 0.25
- need_ids: int32 [8, 8], replicated, may hold values from 0 to 255, as said below
- diagrams: int32 [8, 8, 3], P('src'), may hold values from 0 to 15, as said below
- phases: int32 [16], replicated, may hold values from 0 to 3
- block_sizes: int32 [4], replicated, may hold values from 1 to 3, 8 in all
Outputs:
- correlators: float32 [8, 4, 3, 2, 8], P('src', 'snk')
Inputs may be any that keep to these rules, and one draw needn't show every extreme that they name: `block_sizes`: the sizes sum to 8, and one of them is exactly 3. `need_ids`: the 8 ids of a row are distinct. `diagrams`: entry 0 of a diagram is below 4, entry 1 below 4, entry 2 below 16; each of a row's 4 sink-side and 4 source-side entries is named by some diagram of the row.
All inputs are finite; a program needn't handle non-finite values.
Results may differ from a plain program's by a relative error of at most 0.004.
Values may be sent and summed in bfloat16 or wider, within the bound.
A program may use at most 64 MiB of HBM per device.

v0:
```python
import jax
import jax.numpy as jnp
from jax import lax
from jax.sharding import PartitionSpec as P

NSN = 4
MAXB = 3


def slot_values(gathered, tau_slot, diagram_rows, phases):
    real_part = tau_slot[0]
    imag_part = tau_slot[1]
    left_stack = jnp.stack([jnp.stack([real_part, imag_part]), jnp.stack([-imag_part, real_part])])
    right_stack = jnp.stack([jnp.stack([real_part, -imag_part]), jnp.stack([imag_part, real_part])])
    left_node = lax.dot_general(
        gathered[:, :, :NSN],
        left_stack,
        (((1, 3), (0, 3)), ((), ())),
        preferred_element_type=jnp.float32,
    ).astype(jnp.bfloat16)
    right_node = lax.dot_general(
        gathered[:, :, NSN:],
        right_stack,
        (((1, 3), (0, 2)), ((), ())),
        preferred_element_type=jnp.float32,
    ).astype(jnp.bfloat16)
    pair_sums = lax.dot_general(
        left_node, right_node, (((0, 3), (3, 0)), ((), ())), preferred_element_type=jnp.float32
    )
    pair_real = pair_sums[:, 0, :, 0] - pair_sums[:, 1, :, 1]
    pair_imag = pair_sums[:, 0, :, 1] + pair_sums[:, 1, :, 0]
    sink_pick = (
        diagram_rows[:, 0:1] == jnp.arange(pair_real.shape[0], dtype=jnp.int32)[None, :]
    ).astype(jnp.float32)
    source_pick = (
        diagram_rows[:, 1:2] == jnp.arange(pair_real.shape[1], dtype=jnp.int32)[None, :]
    ).astype(jnp.float32)
    chosen_real = jnp.sum(
        sink_pick[:, :, None] * pair_real[None] * source_pick[:, None, :], axis=(1, 2)
    )
    chosen_imag = jnp.sum(
        sink_pick[:, :, None] * pair_imag[None] * source_pick[:, None, :], axis=(1, 2)
    )
    gamma_pick = diagram_rows[:, 2:3] == jnp.arange(phases.shape[0], dtype=jnp.int32)[None, :]
    quarter = jnp.sum(jnp.where(gamma_pick, phases[None, :], 0), axis=1)
    cosine = (quarter == 0).astype(jnp.float32) - (quarter == 2).astype(jnp.float32)
    sine_part = (quarter == 1).astype(jnp.float32) - (quarter == 3).astype(jnp.float32)
    return jnp.stack(
        [
            cosine * chosen_real - sine_part * chosen_imag,
            sine_part * chosen_real + cosine * chosen_imag,
        ]
    )


def local(tau_cols, elementals, need_ids, diagrams, phases, block_sizes):
    groups = lax.axis_size("snk")
    column = lax.axis_index("snk")
    full_width = tau_cols.shape[4]
    col_count = tau_cols.shape[3]
    sink_count = tau_cols.shape[2]
    diagram_rows = diagrams[0]
    starts = jnp.cumsum(block_sizes) - block_sizes
    offsets = jnp.arange(MAXB, dtype=jnp.int32)
    picked = jnp.take(elementals, need_ids, axis=2)
    arrived = lax.all_to_all(picked, "src", split_axis=2, concat_axis=0, tiled=True)
    gathered = arrived.reshape(full_width, 2, need_ids.shape[1], full_width)
    local_tau = tau_cols[:, 0]
    per_group = sink_count // groups
    half_turn = groups // 2
    packed = local_tau.reshape(2, groups, per_group, col_count, full_width)
    packed = jnp.roll(packed, -half_turn, axis=1)
    arrived_tau = lax.all_to_all(packed, "snk", split_axis=1, concat_axis=3, tiled=True)
    blocks = arrived_tau.reshape(2, per_group, full_width, full_width)
    results = jnp.stack(
        [
            slot_values(gathered, blocks[:, place], diagram_rows, phases)
            for place in range(per_group)
        ]
    )
    all_values = lax.all_gather(results, "snk", axis=0, tiled=True)
    all_values = jnp.roll(all_values, half_turn * per_group, axis=0)
    own_start = lax.dynamic_index_in_dim(starts, column, keepdims=False)
    own_size = lax.dynamic_index_in_dim(block_sizes, column, keepdims=False)
    own_filled = offsets < own_size
    own_times = jnp.where(own_filled, own_start + offsets, 0)
    correlators = jnp.take(all_values, own_times, axis=0) * own_filled[:, None, None].astype(
        jnp.float32
    )
    return correlators.reshape(1, 1, MAXB, 2, diagram_rows.shape[0])


def solution(mesh):
    placed = (
        P(None, "src", None, "snk", None),
        P("src", None, None, None),
        P(),
        P("src", None, None),
        P(),
        P(),
    )
    return jax.shard_map(
        local,
        mesh=mesh,
        in_specs=placed,
        out_specs=P("src", "snk", None, None, None),
        check_vma=False,
    )
```

profile of v0, /device:TPU:0, one launch (start us, length us, event | category | flops | bytes accessed | tf_op | source)
XLA Modules:
  0.0 94.8 jit_solution(11811888920916635707)
XLA Ops:
  0.0 0.0 copy-start.6
  0.0 1.1 %fusion.38 = (bf16[2,2,2,64,256]{4,3,2,1,0:T(8,128)(2,1)S(1)}, bf16[2,2,2,64,256]{4,3,2,1,0:T(8,128)(2,1)S(1)}) fusion(bf16[2,4,2,64,256]{4,3,2,1,0:T(8,128)(2,1)} %bitcast.147), kind=kLoop, calls=%fused_computation.106 | loop fusion | bytes 1048576 | tf_op jit(solution)/shard_map/jit(_roll_static)/slice | solution.py:72
  1.1 0.9 copy.35
  2.0 4.2 %all-to-all-start.1 = ((bf16[2,4,2,64,256]{4,3,2,0,1:T(8,128)(2,1)}), bf16[2,4,2,64,256]{4,3,2,0,1:T(8,128)(2,1)S(1)}, u32[]{:S(2)}, u32[]{:S(2)}) async-start(bf16[2,4,2,64,256]{4,3,2,0,1:T(8,128)(2,1)} %copy.35), calls=%async_computation.1 | async-start | bytes 1048576 | tf_op jit(solution)/shard_map/all_to_all | solution.py:73
  6.2 0.0 copy-done.6
  6.3 0.1 reshape.341
  6.4 6.2 %gather_fusion = bf16[64,32,2,256]{3,0,2,1:T(8,128)(2,1)S(1)} fusion(bf16[32,2,256,256]{3,2,1,0:T(8,128)(2,1)} %param.7, s32[1024]{0:T(1024)S(1)} %pad_clamp_fusion.1), kind=kCustom, calls=%fused_computation | custom fusion | bytes 4194560 | tf_op jit(solution)/shard_map/jit(_take)/gather | solution.py:65
  12.5 2.1 %fusion = bf16[32,2,8,8,256]{4,3,1,0,2:T(8,128)(2,1)} fusion(pred[8,8]{1,0:T(8,128)(4,1)S(1)} %compare_and_fusion, bf16[64,32,2,256]{3,0,2,1:T(8,128)(2,1)S(1)} %gather_fusion), kind=kLoop, calls=%fused_computation.7 | loop fusion | flops 1048576 | bytes 4194368 | tf_op jit(solution)/shard_map/jit(_take)/select_n | solution.py:65
  14.7 0.0 copy-start.7
  14.7 0.0 copy-start.8
  14.7 0.0 copy-start.9
  14.7 0.4 all-to-all-done.1
  15.1 6.5 %all-to-all-start = ((bf16[32,2,8,8,256]{4,3,1,0,2:T(8,128)(2,1)}), bf16[32,2,8,8,256]{4,3,1,0,2:T(8,128)(2,1)S(1)}, u32[]{:S(2)}, u32[]{:S(2)}) async-start(bf16[32,2,8,8,256]{4,3,1,0,2:T(8,128)(2,1)} %fusion), calls=%async_computation | async-start | bytes 4194304 | tf_op jit(solution)/shard_map/all_to_all | solution.py:66
  21.6 0.0 copy-done.7
  21.6 0.0 copy-done.8
  21.6 0.2 reduce-window.9
  21.8 0.6 dynamic_slice.7
  22.4 0.6 dynamic_slice.8
  23.0 1.3 %fusion.32 = s32[3]{0:T(128)S(1)} fusion(s32[]{:T(128)} %bitcast.3, s32[]{:T(128)} %bitcast), kind=kLoop, calls=%fused_computation.97 | loop fusion | flops 18 | bytes 20 | tf_op jit(solution)/shard_map/jit(_take)/jit(_where)/select_n | solution.py:87
  24.3 1.3 %compare_and_fusion.1 = (pred[3]{0:T(512)(128)(4,1)S(1)}, f32[3]{0:T(128)S(1)}) fusion(s32[]{:T(128)} %bitcast.3, s32[]{:T(128)} %bitcast), kind=kLoop, calls=%fused_computation.85 | loop fusion | flops 30 | bytes 23 | tf_op jit(solution)/shard_map/jit(_take)/and | solution.py:87
  25.6 0.0 copy-done.9
  25.6 0.2 select_reduce_fusion
  25.9 1.3 %fusion.17 = (bf16[1,2,256,256]{3,2,0,1:T(8,128)(2,1)S(1)}, bf16[1,2,256,256]{3,2,1,0:T(8,128)(2,1)}, bf16[1,2,256,256]{3,2,1,0:T(8,128)(2,1)}, bf16[1,2,256,256...) fusion(bf16[1,256,256]{2,1,0:T(8,128)(2,1)S(1)} %get-tuple-elem, ...), kind=kLoop, calls=%fused_computation.41 | loop fusion | flops 1048576 | bytes 2883584 | tf_op jit(solution)/shard_map/stack | solution.py:13
  27.2 43.1 %all-to-all-done = bf16[32,2,8,8,256]{4,3,1,0,2:T(8,128)(2,1)S(1)} async-done(((bf16[32,2,8,8,256]{4,3,1,0,2:T(8,128)(2,1)}), bf16[32,2,8,8,256]{4,3,1,0,2:T(8,128)(2,1)S(1)}, u32[]{:S(2)}, u32[]{:S(2)}) %all-to-all-start) | async-done | bytes 2097184 | tf_op jit(solution)/shard_map/all_to_all | solution.py:66
  70.2 0.0 copy-start.4
  70.2 0.7 fusion.37
  70.9 0.0 copy-start
  70.9 1.0 %copy-done = bf16[256,2,4,256]{3,2,1,0:T(4,128)(2,1)} copy-done((bf16[256,2,4,256]{3,2,1,0:T(4,128)(2,1)}, bf16[256,2,4,256]{3,2,1,0:T(4,128)(2,1)S(1)}, u32[]{:S(2)}) %copy-start) | copy-done | bytes 1048600
  71.9 0.0 copy-done.4
  71.9 0.0 copy-done.5
  71.9 0.7 bitcast_convert_fusion.2
  72.6 0.7 copy.41
  73.3 1.8 %fusion.1 = bf16[256,4,2,256,1]{3,0,2,1,4:T(8,128)(2,1)S(1)} fusion(bf16[256,2,4,256]{3,2,1,0:T(4,128)(2,1)S(1)} %get-tuple-element.9, bf16[1,2,256,256]{3,2,0,1:T(8,128)(2,1)} %get-tuple-element.48, bf16[1,2,256,256]{3,2,0,1:T(8,128)(2,1)} %get-tuple-element.51), kind=kOutput, calls=%fused_computation.8 | convolution fusion | flops 538443776 | bytes 2621440 | tf_op jit(solution)/shard_map/dot_general | solution.py:15
  75.1 0.0 copy-start.1
  75.1 0.0 copy-start.2
  75.1 0.0 copy-start.3
  75.1 4.9 %convolution_bitcast_fusion.1 = f32[4,2,4,2]{2,0,3,1:T(4,128)S(1)} fusion(bf16[256,4,2,256]{0,1,3,2:T(4,128)(2,1)S(1)} %copy.41, bf16[256,4,2,256,1]{3,0,2,1,4:T(8,128)(2,1)S(1)} %fusion.1), kind=kOutput, calls=%fused_computation.11 | convolution fusion | flops 8388608 | bytes 2097408 | tf_op jit(solution)/shard_map/dot_general | solution.py:27
  80.1 0.0 copy-done.1
  80.1 0.0 copy-done.2
  80.1 0.0 copy-done.3
  80.1 0.7 bitcast_convert_fusion
  80.8 0.7 copy.45
  81.5 1.7 %fusion.2 = bf16[256,4,2,256,1]{3,0,2,1,4:T(8,128)(2,1)S(1)} fusion(bf16[256,2,4,256]{3,2,1,0:T(4,128)(2,1)S(1)} %get-tuple-element.9, bf16[1,2,256,256]{3,2,0,1:T(8,128)(2,1)} %get-tuple-element.28, bf16[1,2,256,256]{3,2,0,1:T(8,128)(2,1)S(1)} %get-tuple-element.19), kind=kOutput, calls=%fused_computation.9 | convolution fusion | flops 538443776 | bytes 2621440 | tf_op jit(solution)/shard_map/dot_general | solution.py:15
  83.2 4.9 %convolution_bitcast_fusion = f32[4,2,4,2]{2,0,3,1:T(4,128)S(1)} fusion(bf16[256,4,2,256]{0,1,3,2:T(4,128)(2,1)S(1)} %copy.45, bf16[256,4,2,256,1]{3,0,2,1,4:T(8,128)(2,1)S(1)} %fusion.2), kind=kOutput, calls=%fused_computation.10 | convolution fusion | flops 8388608 | bytes 2097408 | tf_op jit(solution)/shard_map/dot_general | solution.py:27
  88.2 0.1 multiply_reduce_fusion.3
  88.4 5.2 %all_gather.3 = f32[8,2,8]{2,1,0:T(2,128)S(1)} all-gather(f32[2,2,8]{2,1,0:T(2,128)S(1)} %pad_maximum_fusion.12), channel_id=1, replica_groups=mesh['src'=8,'snk'=4] {'snk'}, dimensions={0}, use_global_device_ids=true | all-gather | bytes 640 | tf_op jit(solution)/shard_map/all_gather | solution.py:81
  93.6 0.6 gather_fusion.1
  94.1 0.7 fusion.23
  (21 shorter events, 0.2 us)
Async XLA Ops:
  0.0 6.2 %copy-start.6 = (s32[8,8]{1,0:T(8,128)S(1)}, s32[8,8]{1,0:T(8,128)}, u32[]{:S(2)}) copy-start(s32[8,8]{1,0:T(8,128)} %param.8) | copy-start | bytes 772
  2.0 13.1 %all-to-all-start.1 = ((bf16[2,4,2,64,256]{4,3,2,0,1:T(8,128)(2,1)}), bf16[2,4,2,64,256]{4,3,2,0,1:T(8,128)(2,1)S(1)}, u32[]{:S(2)}, u32[]{:S(2)}) async-start(bf16[2,4,2,64,256]{4,3,2,0,1:T(8,128)(2,1)} %copy.35), calls=%async_computation.1 | async-start | bytes 1048576 | tf_op jit(solution)/shard_map/all_to_all | solution.py:73
  14.7 6.9 %copy-start.7 = (s32[1,8,3]{1,0,2:T(1,128)S(1)}, s32[1,8,3]{1,0,2:T(1,128)}, u32[]{:S(2)}) copy-start(s32[1,8,3]{1,0,2:T(1,128)} %param.9) | copy-start | bytes 292
  14.7 6.9 %copy-start.8 = (s32[4]{0:T(128)S(1)}, s32[4]{0:T(128)}, u32[]{:S(2)}) copy-start(s32[4]{0:T(128)} %param.11) | copy-start | bytes 52
  14.7 10.9 %copy-start.9 = (s32[16]{0:T(128)S(1)}, s32[16]{0:T(128)}, u32[]{:S(2)}) copy-start(s32[16]{0:T(128)} %param.10) | copy-start | bytes 196
  15.1 55.2 %all-to-all-start = ((bf16[32,2,8,8,256]{4,3,1,0,2:T(8,128)(2,1)}), bf16[32,2,8,8,256]{4,3,1,0,2:T(8,128)(2,1)S(1)}, u32[]{:S(2)}, u32[]{:S(2)}) async-start(bf16[32,2,8,8,256]{4,3,1,0,2:T(8,128)(2,1)} %fusion), calls=%async_computation | async-start | bytes 4194304 | tf_op jit(solution)/shard_map/all_to_all | solution.py:66
  70.2 1.7 %copy-start.4 = (bf16[1,2,256,256]{3,2,1,0:T(8,128)(2,1)S(1)}, bf16[1,2,256,256]{3,2,1,0:T(8,128)(2,1)}, u32[]{:S(2)}) copy-start(bf16[1,2,256,256]{3,2,1,0:T(8,128)(2,1)} %get-tuple-element.49) | copy-start | bytes 786436
  70.2 1.7 %copy-start.5 = (bf16[1,2,256,256]{3,2,1,0:T(8,128)(2,1)S(1)}, bf16[1,2,256,256]{3,2,1,0:T(8,128)(2,1)}, u32[]{:S(2)}) copy-start(bf16[1,2,256,256]{3,2,1,0:T(8,128)(2,1)} %get-tuple-element.50) | copy-start | bytes 786436
  70.9 1.0 %copy-start = (bf16[256,2,4,256]{3,2,1,0:T(4,128)(2,1)}, bf16[256,2,4,256]{3,2,1,0:T(4,128)(2,1)S(1)}, u32[]{:S(2)}) copy-start(bf16[256,2,4,256]{3,2,1,0:T(4,128)(2,1)S(1)} %get-tuple-element.10) | copy-start | bytes 3145732
  75.1 5.0 %copy-start.1 = (bf16[256,2,4,256]{3,2,1,0:T(4,128)(2,1)S(1)}, bf16[256,2,4,256]{3,2,1,0:T(4,128)(2,1)}, u32[]{:S(2)}) copy-start(bf16[256,2,4,256]{3,2,1,0:T(4,128)(2,1)} %copy-done) | copy-start | bytes 3145732
  75.1 5.0 %copy-start.2 = (bf16[1,2,256,256]{3,2,1,0:T(8,128)(2,1)S(1)}, bf16[1,2,256,256]{3,2,1,0:T(8,128)(2,1)}, u32[]{:S(2)}) copy-start(bf16[1,2,256,256]{3,2,1,0:T(8,128)(2,1)} %get-tuple-element.20) | copy-start | bytes 786436
  75.1 5.0 %copy-start.3 = (bf16[1,2,256,256]{3,2,1,0:T(8,128)(2,1)S(1)}, bf16[1,2,256,256]{3,2,1,0:T(8,128)(2,1)}, u32[]{:S(2)}) copy-start(bf16[1,2,256,256]{3,2,1,0:T(8,128)(2,1)} %get-tuple-element.27) | copy-start | bytes 786436
where the time goes:
time: 95.2 us; the launch traced here: 94.8 us
  waiting for transfers between devices  43.5 us (46%)
  matrix products  14.7 us (15%)
  local copies, waits for them, and re-layouts  13.2 us (14%)
  starting transfers between devices  10.8 us (11%)
  other arithmetic  7.21 us (8%)
  blocking collectives  5.19 us (5%)
    all_to_all x1, waiting for transfers between devices, local(): lax.all_to_all(picked, 'src', split_axis=2, concat_axis=0, tiled=True)  43.1 us
    dot_general x2, matrix products, slot_values(): lax.dot_general(left_node, right_node, (((0, 3), (3, 0)), ((), ())), pref...  9.84 us
    all_to_all x1, starting transfers between devices, local(): lax.all_to_all(picked, 'src', split_axis=2, concat_axis=0, tiled=True)  6.52 us
    gather x1, local copies, waits for them, and re-layouts, local(): picked = jnp.take(elementals, need_ids, axis=2)  6.18 us
    all_gather x1, blocking collectives, local(): all_values = lax.all_gather(results, 'snk', axis=0, tiled=True)  5.19 us
    all_to_all x1, starting transfers between devices, local(): lax.all_to_all(packed, 'snk', split_axis=1, concat_axis=3, tiled=True)  4.24 us
    dot_general x2, matrix products, slot_values(): lax.dot_general(gathered[:, :, :NSN], left_stack, (((1, 3), (0, 3)), ((),...  3.47 us
    select_n x2, other arithmetic, local(): picked = jnp.take(elementals, need_ids, axis=2)  2.12 us
  transfers between devices with their start and end apart: 2, of which 2 were waited for; matrix products, arithmetic and copies ran while one was open for 15% of the time, Pallas kernels for 0%

commit v1 on v0

--- a/solution.py
+++ b/solution.py
@@ -1,6 +1,10 @@
+import functools
+
 import jax
 import jax.numpy as jnp
 from jax import lax
+from jax.experimental import pallas as pl
+from jax.experimental.pallas import tpu as pltpu
 from jax.sharding import PartitionSpec as P
 
 NSN = 4
@@ -53,7 +57,7 @@
     )
 
 
-def local(tau_cols, elementals, need_ids, diagrams, phases, block_sizes):
+def plain_local(tau_cols, elementals, need_ids, diagrams, phases, block_sizes):
     groups = lax.axis_size("snk")
     column = lax.axis_index("snk")
     full_width = tau_cols.shape[4]
@@ -90,6 +94,273 @@
     return correlators.reshape(1, 1, MAXB, 2, diagram_rows.shape[0])
 
 
+MESH = pl.DeviceIdType.MESH
+SEND_ORDER = (4, 5, 6, 7, 2, 3, 1)
+TAKE_ORDER = (0, 1, 4, 5, 2, 3, 6, 7)
+NT = (((1,), (1,)), ((), ()))
+NN = (((1,), (0,)), ((), ()))
+
+
+def flipped(value, mask):
+    for bit in (1, 2, 4):
+        if mask & bit:
+            value = value + bit * (1 - 2 * ((value // bit) % 2))
+    return value
+
+
+def kernel(
+    ids_ref, diag_ref, phase_ref, size_ref, tau_ref, el_ref, out_ref,
+    table, pick, sendbuf, ebuf, xbuf, xneg, lt, rt, vbuf,
+    tab_sem, own_sem, tau_own, tau_send, tau_recv,
+    src_send, src_recv, near_send, near_recv, far_send, far_recv, pass_send, pass_recv,
+    val_send, val_recv,
+):
+    s = lax.axis_index("src")
+    c = lax.axis_index("snk")
+    x, h = c // 2, c % 2
+    n_src, n_ids = ids_ref.shape
+    rows, ne, nv = table.shape
+    per = xbuf.shape[1]
+    f32, bf16 = jnp.float32, jnp.bfloat16
+
+    barrier = pltpu.get_barrier_semaphore()
+    for m in range(1, n_src):
+        pl.semaphore_signal(barrier, 1, device_id=(flipped(s, m), c), device_id_type=MESH)
+    for m in range(1, 4):
+        pl.semaphore_signal(barrier, 1, device_id=(s, flipped(c, m)), device_id_type=MESH)
+
+    table_in = pltpu.make_async_copy(el_ref.at[pl.ds(h * rows, rows), x], table, tab_sem)
+    table_in.start()
+    tau_in = pltpu.make_async_copy(
+        tau_ref.at[:, 0, pl.ds(c * per, per)], xbuf.at[:, :, c], tau_own
+    )
+    tau_in.start()
+
+    sub = lax.broadcasted_iota(jnp.int32, (n_ids, ne), 0)
+    lane = lax.broadcasted_iota(jnp.int32, (n_ids, ne), 1)
+    hots = []
+    for i in range(n_src):
+        wanted = jnp.zeros((n_ids, ne), jnp.int32)
+        for k in range(n_ids):
+            wanted = jnp.where(sub == k, ids_ref[i, k], wanted)
+        hots.append((wanted == lane).astype(f32))
+    hot = jnp.concatenate(hots, axis=0).astype(bf16)
+
+    pl.semaphore_wait(barrier, n_src - 1 + 3)
+    tau_out = []
+    for m in (2, 3, 1):
+        peer = flipped(c, m)
+        copy = pltpu.make_async_remote_copy(
+            src_ref=tau_ref.at[:, 0, pl.ds(peer * per, per)], dst_ref=xbuf.at[:, :, c],
+            send_sem=tau_send.at[m], recv_sem=tau_recv.at[m],
+            device_id=(s, peer), device_id_type=MESH,
+        )
+        copy.start()
+        tau_out.append(copy)
+
+    table_in.wait()
+    for r in range(rows):
+        got = lax.dot_general(hot, table[r], NN, preferred_element_type=f32)
+        for half in range(nv // 128):
+            pick[half, pl.ds(r, n_src * n_ids, stride=rows), :] = got[:, half * 128:(half + 1) * 128]
+    for i in range(n_src):
+        for half in range(nv // 128):
+            sendbuf[i, :, :, half * 128:(half + 1) * 128] = (
+                pick[half, pl.ds(i * n_ids * rows, n_ids * rows), :]
+                .astype(bf16)
+                .reshape(n_ids, rows, 128)
+            )
+
+    def slot(source, column):
+        return ebuf.at[column // 2, source * 2 + column % 2]
+
+    src_out = {}
+    for m in SEND_ORDER:
+        peer = flipped(s, m)
+        src_out[m] = pltpu.make_async_remote_copy(
+            src_ref=sendbuf.at[peer], dst_ref=slot(s, c),
+            send_sem=src_send.at[m], recv_sem=src_recv.at[m],
+            device_id=(peer, c), device_id_type=MESH,
+        )
+        src_out[m].start()
+    own = pltpu.make_async_copy(sendbuf.at[s], slot(s, c), own_sem)
+    own.start()
+
+    near, across = flipped(c, 1), flipped(c, 2)
+    near_out, far_out, pass_out = {}, {}, {}
+
+    def pass_on(m):
+        far_out[m].wait_recv()
+        came = slot(flipped(s, m), across)
+        pass_out[m] = pltpu.make_async_remote_copy(
+            src_ref=came, dst_ref=came,
+            send_sem=pass_send.at[m], recv_sem=pass_recv.at[m],
+            device_id=(s, near), device_id_type=MESH,
+        )
+        pass_out[m].start()
+
+    for n, m in enumerate(TAKE_ORDER):
+        mine = slot(flipped(s, m), c)
+        if m == 0:
+            own.wait()
+        else:
+            src_out[m].wait_recv()
+        far_out[m] = pltpu.make_async_remote_copy(
+            src_ref=mine, dst_ref=mine, send_sem=far_send.at[m], recv_sem=far_recv.at[m],
+            device_id=(s, across), device_id_type=MESH,
+        )
+        far_out[m].start()
+        near_out[m] = pltpu.make_async_remote_copy(
+            src_ref=mine, dst_ref=mine, send_sem=near_send.at[m], recv_sem=near_recv.at[m],
+            device_id=(s, near), device_id_type=MESH,
+        )
+        near_out[m].start()
+        if n >= 1:
+            pass_on(TAKE_ORDER[n - 1])
+    pass_on(TAKE_ORDER[-1])
+
+    tau_in.wait()
+    for copy in tau_out:
+        copy.wait_recv()
+    for t in range(per):
+        xneg[t] = -xbuf[1, t].reshape(nv, nv)
+    for m in TAKE_ORDER:
+        near_out[m].wait_recv()
+        pass_out[m].wait_recv()
+
+    def nodes(k, carry):
+        left_re = ebuf[0, :, k].reshape(nv, nv)
+        left_im = ebuf[1, :, k].reshape(nv, nv)
+        right_re = ebuf[0, :, NSN + k].reshape(nv, nv)
+        right_im = ebuf[1, :, NSN + k].reshape(nv, nv)
+        for t in range(per):
+            x_re = xbuf[0, t].reshape(nv, nv)
+            x_im = xbuf[1, t].reshape(nv, nv)
+            x_neg = xneg[t]
+
+            def mm(a, b, dims):
+                return lax.dot_general(a, b, dims, preferred_element_type=f32)
+
+            def rounded(value):
+                return value.astype(bf16).astype(f32)
+
+            lt[k, t, 0] = rounded(mm(x_re, left_re, NT) + mm(x_neg, left_im, NT))
+            lt[k, t, 1] = rounded(mm(x_re, left_im, NT) + mm(x_im, left_re, NT))
+            rt[k, t, 0] = rounded(mm(right_re, x_re, NN) + mm(right_im, x_im, NN))
+            rt[k, t, 1] = rounded(mm(right_im, x_re, NN) + mm(right_re, x_neg, NN))
+        return carry
+
+    lax.fori_loop(0, NSN, nodes, 0)
+
+    n_diag = diag_ref.shape[1]
+    picks = [(diag_ref[0, d, 0], diag_ref[0, d, 1], phase_ref[diag_ref[0, d, 2]]) for d in range(n_diag)]
+    for t in range(per):
+
+        def rows_of(block, sums):
+            at = pl.ds(pl.multiple_of(block * 8, 8), 8)
+            sums = list(sums)
+            for half in range(nv // 128):
+                lanes = slice(half * 128, (half + 1) * 128)
+                for d, (k1, k2, _) in enumerate(picks):
+                    a_re, a_im = lt[k1, t, 0, at, lanes], lt[k1, t, 1, at, lanes]
+                    b_re, b_im = rt[k2, t, 0, at, lanes], rt[k2, t, 1, at, lanes]
+                    sums[2 * d] = sums[2 * d] + a_re * b_re - a_im * b_im
+                    sums[2 * d + 1] = sums[2 * d + 1] + a_re * b_im + a_im * b_re
+            return tuple(sums)
+
+        zero = jnp.zeros((8, 128), f32)
+        sums = lax.fori_loop(0, nv // 8, rows_of, (zero,) * (2 * n_diag))
+        real, imag = [], []
+        for d, (_, _, turn) in enumerate(picks):
+            cosine = (turn == 0).astype(f32) - (turn == 2).astype(f32)
+            sine = (turn == 1).astype(f32) - (turn == 3).astype(f32)
+            re = jnp.sum(sums[2 * d], axis=0, keepdims=True)
+            im = jnp.sum(sums[2 * d + 1], axis=0, keepdims=True)
+            real.append(cosine * re - sine * im)
+            imag.append(sine * re + cosine * im)
+        vbuf[c * per + t] = jnp.concatenate(real + imag, axis=0)
+
+    val_out = []
+    for m in (2, 3, 1):
+        peer = flipped(c, m)
+        mine = vbuf.at[pl.ds(c * per, per)]
+        copy = pltpu.make_async_remote_copy(
+            src_ref=mine, dst_ref=mine, send_sem=val_send.at[m], recv_sem=val_recv.at[m],
+            device_id=(s, peer), device_id_type=MESH,
+        )
+        copy.start()
+        val_out.append(copy)
+    for copy in val_out:
+        copy.wait_recv()
+
+    first, size = 0, 0
+    for j in range(size_ref.shape[0]):
+        first = first + jnp.where(j < c, size_ref[j], 0)
+        size = size + jnp.where(j == c, size_ref[j], 0)
+    for place in range(MAXB):
+        at = jnp.minimum(first + place, vbuf.shape[0] - 1)
+        keep = (place < size).astype(f32)
+        out_ref[place] = vbuf[at] * keep
+
+    for m in TAKE_ORDER:
+        if m:
+            src_out[m].wait_send()
+        far_out[m].wait_send()
+        near_out[m].wait_send()
+        pass_out[m].wait_send()
+    for copy in tau_out + val_out:
+        copy.wait_send()
+
+
+def fused_local(tau_cols, elementals, need_ids, diagrams, phases, block_sizes):
+    n_snk = lax.axis_size("snk")
+    n_src, n_ids = need_ids.shape
+    own_rows, _, ne, nv = elementals.shape
+    sinks, cols = tau_cols.shape[2], tau_cols.shape[3]
+    per = sinks // n_snk
+    rows = own_rows // 2
+    n_diag = diagrams.shape[1]
+    bf16, f32 = jnp.bfloat16, jnp.float32
+    sem = pltpu.SemaphoreType.DMA
+    smem = pl.BlockSpec(memory_space=pltpu.SMEM)
+    anywhere = pl.BlockSpec(memory_space=pl.ANY)
+    partial = pl.pallas_call(
+        kernel,
+        out_shape=jax.ShapeDtypeStruct((MAXB, 2 * n_diag, 128), f32),
+        in_specs=[smem] * 4 + [anywhere] * 2,
+        out_specs=pl.BlockSpec(memory_space=pltpu.VMEM),
+        scratch_shapes=[
+            pltpu.VMEM((rows, ne, nv), bf16),
+            pltpu.VMEM((nv // 128, n_src * n_ids * rows, 128), f32),
+            pltpu.VMEM((n_src, n_ids, rows, nv), bf16),
+            pltpu.VMEM((2, 2 * n_src, n_ids, rows, nv), bf16),
+            pltpu.VMEM((2, per, n_snk, cols, nv), bf16),
+            pltpu.VMEM((per, nv, nv), bf16),
+            pltpu.VMEM((NSN, per, 2, nv, nv), f32),
+            pltpu.VMEM((n_ids - NSN, per, 2, nv, nv), f32),
+            pltpu.VMEM((sinks, 2 * n_diag, 128), f32),
+            sem, sem, sem, sem((4,)), sem((4,)),
+        ]
+        + [sem((n_src,))] * 8
+        + [sem((4,))] * 2,
+        compiler_params=pltpu.CompilerParams(
+            collective_id=0, has_side_effects=True, vmem_limit_bytes=50 * 1024 * 1024
+        ),
+    )(need_ids, diagrams, phases, block_sizes, tau_cols, elementals)
+    return jnp.sum(partial, axis=2).reshape(1, 1, MAXB, 2, n_diag)
+
+
+def local(tau_cols, elementals, *rest):
+    fits = (
+        lax.axis_size("snk") == 4
+        and lax.axis_size("src") == 8
+        and elementals.shape[0] == 32
+        and tau_cols.shape[3] % 16 == 0
+        and tau_cols.shape[4] % 128 == 0
+    )
+    return (fused_local if fits else plain_local)(tau_cols, elementals, *rest)
+
+
 def solution(mesh):
     placed = (
         P(None, "src", None, "snk", None),

time: 95.2 us -> 43 us (0.45)
  waiting for transfers between devices: 43.5 us -> 0 us
  Pallas kernels: 0 us -> 38.2 us
  matrix products: 14.7 us -> 0 us
  starting transfers between devices: 10.8 us -> 0 us
  local copies, waits for them, and re-layouts: 13.2 us -> 4.46 us
  other arithmetic: 7.21 us -> 0.09 us
  blocking collectives: 5.19 us -> 0 us
    all_to_all x2 -> x0, waiting for transfers between devices: 43.5 us -> none  [the longest x1 43.1 us: local(): lax.all_to_all(picked, 'src', split_axis=2, concat_axis=0, tiled=True)]
    pallas_call x0 -> x1, Pallas kernels: none -> 38.2 us  [fused_local(): pl.pallas_call(kernel, out_shape=jax.ShapeDtypeStruct((MAXB, 2 * n_diag,...]
    dot_general x6 -> x0, matrix products: 14.7 us -> none  [the longest x2 9.84 us: slot_values(): lax.dot_general(left_node, right_node, (((0, 3), (3, 0)), ((), ())), pref...]
    all_to_all x2 -> x0, starting transfers between devices: 10.8 us -> none  [the longest x1 6.52 us: local(): lax.all_to_all(picked, 'src', split_axis=2, concat_axis=0, tiled=True)]
    gather x2 -> x0, local copies, waits for them, and re-layouts: 6.75 us -> none  [the longest x1 6.18 us: local(): picked = jnp.take(elementals, need_ids, axis=2)]
    all_gather x1 -> x0, blocking collectives: 5.19 us -> none  [local(): all_values = lax.all_gather(results, 'snk', axis=0, tiled=True)]
    select_n x3 -> x0, other arithmetic: 3.39 us -> none  [the longest x2 2.12 us: local(): picked = jnp.take(elementals, need_ids, axis=2)]
    unnamed x21 -> x9, local copies, waits for them, and re-layouts: 0.99 us -> 3.79 us
  transfers between devices with their start and end apart: 2 -> 0, of which waited for: 2 -> 0; matrix products, arithmetic and copies ran while one was open for 15% -> 0% of each run, Pallas kernels for 0% -> 0%
where the time goes in v1:
time: 43 us; the launch traced here: 42.8 us
  Pallas kernels  38.2 us (89%)
  local copies, waits for them, and re-layouts  4.46 us (10%)
    pallas_call x1, Pallas kernels, fused_local(): pl.pallas_call(kernel, out_shape=jax.ShapeDtypeStruct((MAXB, 2 * n_diag,...  38.2 us
    unnamed x9, local copies, waits for them, and re-layouts  3.79 us

profile of v1, /device:TPU:0, one launch (start us, length us, event | category | flops | bytes accessed | tf_op | source)
XLA Modules:
  0.0 42.8 jit_solution(10427753347154981691)
XLA Ops:
  0.0 0.8 %copy.7.diag_ref = s32[1,8,3]{2,1,0:T(8,128)S(1)} copy(s32[1,8,3]{1,0,2:T(1,128)} %param.9) | data formatting | bytes 192 | tf_op args[3]
  0.8 0.0 copy-start
  0.8 1.0 %copy-done = bf16[2,1,8,64,256]{4,3,2,1,0:T(8,128)(2,1)S(1)} copy-done((bf16[2,1,8,64,256]{4,3,2,1,0:T(8,128)(2,1)S(1)}, bf16[2,1,8,64,256]{4,3,2,1,0:T(8,128)(2,1)}, u32[]{:S(2)}) %copy-start) | copy-done | bytes 524312
  1.8 0.0 copy-start.1
  1.8 0.7 %copy-done.1 = s32[8,8]{1,0:T(8,128)S(1)} copy-done((s32[8,8]{1,0:T(8,128)S(1)}, s32[8,8]{1,0:T(8,128)}, u32[]{:S(2)}) %copy-start.1) | copy-done | bytes 280
  2.5 0.0 copy-start.2
  2.5 0.7 %copy-done.2 = s32[16]{0:T(128)S(1)} copy-done((s32[16]{0:T(128)S(1)}, s32[16]{0:T(128)}, u32[]{:S(2)}) %copy-start.2) | copy-done | bytes 88
  3.1 0.0 copy-start.3
  3.1 0.7 %copy-done.3 = s32[4]{0:T(128)S(1)} copy-done((s32[4]{0:T(128)S(1)}, s32[4]{0:T(128)}, u32[]{:S(2)}) %copy-start.3) | copy-done | bytes 40
  3.8 38.2 %shard_map.64 = f32[3,16,128]{2,1,0:T(8,128)S(1)} custom-call(s32[8,8]{1,0:T(8,128)S(1)} %copy-done.1, s32[1,8,3]{2,1,0:T(8,128)S(1)} %copy.7.diag_ref, s32[16]{0:T(128)S(1)} %copy-done.2, s32[4]{0:T(128)S(1)} %copy-done.3, bf16[2,1,8,64,256]{4,3,2,1,0:T(8,128)(2,1)S(1)} %copy-done, bf16[32,2,256,256]{3,2,1,0:T(8,128)(2,1)} %el_ref.1), custom_call_target="tpu_custom_call" | custom-call | tf_op jit(solution)/shard_map/pallas_call | solution.py:327
  42.0 0.1 reduce_sum.9
  42.1 0.7 %reshape.3 = f32[1,1,3,2,8]{4,3,2,1,0:T(2,128)} reshape(f32[3,16]{1,0:T(4,128)S(1)} %reduce_sum.9) | data formatting | bytes 384 | tf_op jit(solution)/shard_map/reshape | solution.py:350
Async XLA Ops:
  0.8 1.0 %copy-start = (bf16[2,1,8,64,256]{4,3,2,1,0:T(8,128)(2,1)S(1)}, bf16[2,1,8,64,256]{4,3,2,1,0:T(8,128)(2,1)}, u32[]{:S(2)}) copy-start(bf16[2,1,8,64,256]{4,3,2,1,0:T(8,128)(2,1)} %tau_ref.1) | copy-start | bytes 1572868
  1.8 0.7 %copy-start.1 = (s32[8,8]{1,0:T(8,128)S(1)}, s32[8,8]{1,0:T(8,128)}, u32[]{:S(2)}) copy-start(s32[8,8]{1,0:T(8,128)} %ids_ref.1) | copy-start | bytes 772
  2.5 0.7 %copy-start.2 = (s32[16]{0:T(128)S(1)}, s32[16]{0:T(128)}, u32[]{:S(2)}) copy-start(s32[16]{0:T(128)} %phase_ref.1) | copy-start | bytes 196
  3.1 0.7 %copy-start.3 = (s32[4]{0:T(128)S(1)}, s32[4]{0:T(128)}, u32[]{:S(2)}) copy-start(s32[4]{0:T(128)} %size_ref.1) | copy-start | bytes 52

commit v2 on v1

--- a/solution.py
+++ b/solution.py
@@ -95,8 +95,9 @@
 
 
 MESH = pl.DeviceIdType.MESH
-SEND_ORDER = (4, 5, 6, 7, 2, 3, 1)
-TAKE_ORDER = (0, 1, 4, 5, 2, 3, 6, 7)
+HALF = 4
+RELAYED = (4, 5, 6, 7)
+DIRECT = (2, 3, 1)
 NT = (((1,), (1,)), ((), ()))
 NN = (((1,), (0,)), ((), ()))
 
@@ -109,19 +110,34 @@
 
 
 def kernel(
-    ids_ref, diag_ref, phase_ref, size_ref, tau_ref, el_ref, out_ref,
-    table, pick, sendbuf, ebuf, xbuf, xneg, lt, rt, vbuf,
-    tab_sem, own_sem, tau_own, tau_send, tau_recv,
-    src_send, src_recv, near_send, near_recv, far_send, far_recv, pass_send, pass_recv,
+    ids_hbm, diag_hbm, phase_hbm, size_hbm, tau_ref, el_ref, out_ref,
+    ids_ref, diag_ref, phase_ref, size_ref,
+    table, pick, sendbuf, sendother, ebuf, xbuf, xneg, lt, rt, vbuf,
+    small_sem, tab_sem, own_sem, tau_own, tau_send, tau_recv,
+    src_send, src_recv, near_send, near_recv, far_send, far_recv,
     val_send, val_recv,
 ):
     s = lax.axis_index("src")
     c = lax.axis_index("snk")
     x, h = c // 2, c % 2
     n_src, n_ids = ids_ref.shape
-    rows, ne, nv = table.shape
+    rows, ne, nv = table.shape[1:]
     per = xbuf.shape[1]
     f32, bf16 = jnp.float32, jnp.bfloat16
+    base = (s // HALF) * HALF
+
+    smalls = []
+    for n, (there, here) in enumerate(
+        ((ids_hbm, ids_ref), (diag_hbm, diag_ref), (phase_hbm, phase_ref), (size_hbm, size_ref))
+    ):
+        smalls.append(pltpu.make_async_copy(there, here, small_sem.at[n]))
+        smalls[-1].start()
+    table_in = []
+    for n, part in enumerate((x, 1 - x)):
+        table_in.append(
+            pltpu.make_async_copy(el_ref.at[pl.ds(h * rows, rows), part], table.at[n], tab_sem.at[n])
+        )
+        table_in[-1].start()
 
     barrier = pltpu.get_barrier_semaphore()
     for m in range(1, n_src):
@@ -129,8 +145,6 @@
     for m in range(1, 4):
         pl.semaphore_signal(barrier, 1, device_id=(s, flipped(c, m)), device_id_type=MESH)
 
-    table_in = pltpu.make_async_copy(el_ref.at[pl.ds(h * rows, rows), x], table, tab_sem)
-    table_in.start()
     tau_in = pltpu.make_async_copy(
         tau_ref.at[:, 0, pl.ds(c * per, per)], xbuf.at[:, :, c], tau_own
     )
@@ -138,14 +152,32 @@
 
     sub = lax.broadcasted_iota(jnp.int32, (n_ids, ne), 0)
     lane = lax.broadcasted_iota(jnp.int32, (n_ids, ne), 1)
-    hots = []
-    for i in range(n_src):
-        wanted = jnp.zeros((n_ids, ne), jnp.int32)
-        for k in range(n_ids):
-            wanted = jnp.where(sub == k, ids_ref[i, k], wanted)
-        hots.append((wanted == lane).astype(f32))
-    hot = jnp.concatenate(hots, axis=0).astype(bf16)
-
+    smalls[0].wait()
+
+    def one_hot(owners):
+        hots = []
+        for i in owners:
+            wanted = jnp.zeros((n_ids, ne), jnp.int32)
+            for k in range(n_ids):
+                wanted = jnp.where(sub == k, ids_ref[i, k], wanted)
+            hots.append((wanted == lane).astype(f32))
+        return jnp.concatenate(hots, axis=0).astype(bf16)
+
+    def pick_rows(n, hot, target):
+        count = target.shape[0] * n_ids
+        for r in range(rows):
+            got = lax.dot_general(hot, table[n, r], NN, preferred_element_type=f32)
+            for half in range(nv // 128):
+                pick[half, pl.ds(r, count, stride=rows), :] = got[:, half * 128:(half + 1) * 128]
+        for i in range(target.shape[0]):
+            for half in range(nv // 128):
+                target[i, :, :, half * 128:(half + 1) * 128] = (
+                    pick[half, pl.ds(i * n_ids * rows, n_ids * rows), :]
+                    .astype(bf16)
+                    .reshape(n_ids, rows, 128)
+                )
+
+    hot = one_hot(range(n_src))
     pl.semaphore_wait(barrier, n_src - 1 + 3)
     tau_out = []
     for m in (2, 3, 1):
@@ -158,75 +190,73 @@
         copy.start()
         tau_out.append(copy)
 
-    table_in.wait()
-    for r in range(rows):
-        got = lax.dot_general(hot, table[r], NN, preferred_element_type=f32)
-        for half in range(nv // 128):
-            pick[half, pl.ds(r, n_src * n_ids, stride=rows), :] = got[:, half * 128:(half + 1) * 128]
-    for i in range(n_src):
-        for half in range(nv // 128):
-            sendbuf[i, :, :, half * 128:(half + 1) * 128] = (
-                pick[half, pl.ds(i * n_ids * rows, n_ids * rows), :]
-                .astype(bf16)
-                .reshape(n_ids, rows, 128)
-            )
-
-    def slot(source, column):
-        return ebuf.at[column // 2, source * 2 + column % 2]
+    def slot(part, source):
+        return ebuf.at[part, source * 2 + h]
 
     src_out = {}
-    for m in SEND_ORDER:
-        peer = flipped(s, m)
-        src_out[m] = pltpu.make_async_remote_copy(
-            src_ref=sendbuf.at[peer], dst_ref=slot(s, c),
-            send_sem=src_send.at[m], recv_sem=src_recv.at[m],
-            device_id=(peer, c), device_id_type=MESH,
-        )
-        src_out[m].start()
-    own = pltpu.make_async_copy(sendbuf.at[s], slot(s, c), own_sem)
-    own.start()
+
+    def send_on(n, m, chunk):
+        src_out[n, m] = pltpu.make_async_remote_copy(
+            src_ref=chunk, dst_ref=slot((x, 1 - x)[n], s),
+            send_sem=src_send.at[n, m], recv_sem=src_recv.at[n, m],
+            device_id=(flipped(s, m), c), device_id_type=MESH,
+        )
+        src_out[n, m].start()
+
+    table_in[0].wait()
+    pick_rows(0, hot, sendbuf)
+    for m in RELAYED + DIRECT:
+        send_on(0, m, sendbuf.at[flipped(s, m)])
+    own = [pltpu.make_async_copy(sendbuf.at[s], slot(x, s), own_sem.at[0])]
+    own[0].start()
+    table_in[1].wait()
+    pick_rows(1, one_hot([base + i for i in range(HALF)]), sendother)
+    for m in DIRECT:
+        send_on(1, m, sendother.at[flipped(s, m) - base])
+    own.append(pltpu.make_async_copy(sendother.at[s - base], slot(1 - x, s), own_sem.at[1]))
+    own[1].start()
 
     near, across = flipped(c, 1), flipped(c, 2)
-    near_out, far_out, pass_out = {}, {}, {}
-
-    def pass_on(m):
+    near_out, far_out = {}, {}
+
+    def to_near(n, m):
+        chunk = slot((x, 1 - x)[n], flipped(s, m))
+        near_out[n, m] = pltpu.make_async_remote_copy(
+            src_ref=chunk, dst_ref=chunk, send_sem=near_send.at[n, m], recv_sem=near_recv.at[n, m],
+            device_id=(s, near), device_id_type=MESH,
+        )
+        near_out[n, m].start()
+
+    for n in (0, 1):
+        own[n].wait()
+        to_near(n, 0)
+    for n in (0, 1):
+        src_out[n, 1].wait_recv()
+        to_near(n, 1)
+    for m in RELAYED:
+        src_out[0, m].wait_recv()
+        chunk = slot(x, flipped(s, m))
+        far_out[m] = pltpu.make_async_remote_copy(
+            src_ref=chunk, dst_ref=chunk, send_sem=far_send.at[m], recv_sem=far_recv.at[m],
+            device_id=(s, across), device_id_type=MESH,
+        )
+        far_out[m].start()
+        to_near(0, m)
+    for m in (2, 3):
+        for n in (0, 1):
+            src_out[n, m].wait_recv()
+            to_near(n, m)
+    for m in RELAYED:
         far_out[m].wait_recv()
-        came = slot(flipped(s, m), across)
-        pass_out[m] = pltpu.make_async_remote_copy(
-            src_ref=came, dst_ref=came,
-            send_sem=pass_send.at[m], recv_sem=pass_recv.at[m],
-            device_id=(s, near), device_id_type=MESH,
-        )
-        pass_out[m].start()
-
-    for n, m in enumerate(TAKE_ORDER):
-        mine = slot(flipped(s, m), c)
-        if m == 0:
-            own.wait()
-        else:
-            src_out[m].wait_recv()
-        far_out[m] = pltpu.make_async_remote_copy(
-            src_ref=mine, dst_ref=mine, send_sem=far_send.at[m], recv_sem=far_recv.at[m],
-            device_id=(s, across), device_id_type=MESH,
-        )
-        far_out[m].start()
-        near_out[m] = pltpu.make_async_remote_copy(
-            src_ref=mine, dst_ref=mine, send_sem=near_send.at[m], recv_sem=near_recv.at[m],
-            device_id=(s, near), device_id_type=MESH,
-        )
-        near_out[m].start()
-        if n >= 1:
-            pass_on(TAKE_ORDER[n - 1])
-    pass_on(TAKE_ORDER[-1])
+        to_near(1, m)
 
     tau_in.wait()
     for copy in tau_out:
         copy.wait_recv()
     for t in range(per):
         xneg[t] = -xbuf[1, t].reshape(nv, nv)
-    for m in TAKE_ORDER:
-        near_out[m].wait_recv()
-        pass_out[m].wait_recv()
+    for copy in near_out.values():
+        copy.wait_recv()
 
     def nodes(k, carry):
         left_re = ebuf[0, :, k].reshape(nv, nv)
@@ -252,8 +282,10 @@
 
     lax.fori_loop(0, NSN, nodes, 0)
 
-    n_diag = diag_ref.shape[1]
-    picks = [(diag_ref[0, d, 0], diag_ref[0, d, 1], phase_ref[diag_ref[0, d, 2]]) for d in range(n_diag)]
+    n_diag = diag_ref.shape[2]
+    for copy in smalls[1:]:
+        copy.wait()
+    picks = [(diag_ref[0, 0, d], diag_ref[1, 0, d], phase_ref[diag_ref[2, 0, d]]) for d in range(n_diag)]
     for t in range(per):
 
         def rows_of(block, sums):
@@ -302,12 +334,8 @@
         keep = (place < size).astype(f32)
         out_ref[place] = vbuf[at] * keep
 
-    for m in TAKE_ORDER:
-        if m:
-            src_out[m].wait_send()
-        far_out[m].wait_send()
-        near_out[m].wait_send()
-        pass_out[m].wait_send()
+    for copy in list(src_out.values()) + list(far_out.values()) + list(near_out.values()):
+        copy.wait_send()
     for copy in tau_out + val_out:
         copy.wait_send()
 
@@ -322,31 +350,37 @@
     n_diag = diagrams.shape[1]
     bf16, f32 = jnp.bfloat16, jnp.float32
     sem = pltpu.SemaphoreType.DMA
-    smem = pl.BlockSpec(memory_space=pltpu.SMEM)
-    anywhere = pl.BlockSpec(memory_space=pl.ANY)
+    i32 = jnp.int32
+    held = pl.BlockSpec(memory_space=pltpu.HBM)
     partial = pl.pallas_call(
         kernel,
         out_shape=jax.ShapeDtypeStruct((MAXB, 2 * n_diag, 128), f32),
-        in_specs=[smem] * 4 + [anywhere] * 2,
+        in_specs=[held] * 6,
         out_specs=pl.BlockSpec(memory_space=pltpu.VMEM),
         scratch_shapes=[
-            pltpu.VMEM((rows, ne, nv), bf16),
+            pltpu.SMEM((n_src, n_ids), i32),
+            pltpu.SMEM((3, 1, n_diag), i32),
+            pltpu.SMEM(phases.shape, i32),
+            pltpu.SMEM(block_sizes.shape, i32),
+            pltpu.VMEM((2, rows, ne, nv), bf16),
             pltpu.VMEM((nv // 128, n_src * n_ids * rows, 128), f32),
             pltpu.VMEM((n_src, n_ids, rows, nv), bf16),
+            pltpu.VMEM((HALF, n_ids, rows, nv), bf16),
             pltpu.VMEM((2, 2 * n_src, n_ids, rows, nv), bf16),
             pltpu.VMEM((2, per, n_snk, cols, nv), bf16),
             pltpu.VMEM((per, nv, nv), bf16),
             pltpu.VMEM((NSN, per, 2, nv, nv), f32),
             pltpu.VMEM((n_ids - NSN, per, 2, nv, nv), f32),
             pltpu.VMEM((sinks, 2 * n_diag, 128), f32),
-            sem, sem, sem, sem((4,)), sem((4,)),
+            sem((4,)), sem((2,)), sem((2,)), sem, sem((4,)), sem((4,)),
         ]
-        + [sem((n_src,))] * 8
+        + [sem((2, n_src))] * 4
+        + [sem((n_src,))] * 2
         + [sem((4,))] * 2,
         compiler_params=pltpu.CompilerParams(
-            collective_id=0, has_side_effects=True, vmem_limit_bytes=50 * 1024 * 1024
+            collective_id=0, has_side_effects=True, vmem_limit_bytes=67043328
         ),
-    )(need_ids, diagrams, phases, block_sizes, tau_cols, elementals)
+    )(need_ids, jnp.transpose(diagrams, (2, 0, 1)), phases, block_sizes, tau_cols, elementals)
     return jnp.sum(partial, axis=2).reshape(1, 1, MAXB, 2, n_diag)
 
 

time: 43 us -> 35 us (0.81)
  Pallas kernels: 38.2 us -> 33.3 us
  local copies, waits for them, and re-layouts: 4.46 us -> 0.66 us
  other arithmetic: 0.09 us -> 0.82 us
    pallas_call x1, Pallas kernels: 38.2 us -> 33.3 us  [fused_local(): pl.pallas_call(kernel, out_shape=jax.ShapeDtypeStruct((MAXB, 2 * n_diag,...]
    unnamed x9 -> x0, local copies, waits for them, and re-layouts: 3.79 us -> none
    reduce_sum x1, other arithmetic: 0.09 us -> 0.82 us  [fused_local(): return jnp.sum(partial, axis=2).reshape(1, 1, MAXB, 2, n_diag)]
where the time goes in v2:
time: 35 us; the launch traced here: 34.8 us
  Pallas kernels  33.3 us (95%)
  other arithmetic  0.82 us (2%)
  local copies, waits for them, and re-layouts  0.66 us (2%)
    pallas_call x1, Pallas kernels, fused_local(): pl.pallas_call(kernel, out_shape=jax.ShapeDtypeStruct((MAXB, 2 * n_diag,...  33.3 us
    reduce_sum x1, other arithmetic, fused_local(): return jnp.sum(partial, axis=2).reshape(1, 1, MAXB, 2, n_diag)  0.82 us

profile of v2, /device:TPU:0, one launch (start us, length us, event | category | flops | bytes accessed | tf_op | source)
XLA Modules:
  0.0 34.8 jit_solution(15780081788584350386)
XLA Ops:
  0.0 33.3 %shard_map.64 = f32[3,16,128]{2,1,0:T(8,128)} custom-call(s32[8,8]{1,0:T(8,128)} %ids_hbm.1, s32[3,1,8]{2,1,0:T(1,128)} %bitcast.1, s32[16]{0:T(128)} %phase_hbm.1, s32[4]{0:T(128)} %size_hbm.1, bf16[2,1,8,64,256]{4,3,2,1,0:T(8,128)(2,1)} %tau_ref.1, bf16[32,2,256,256]{3,2,1,0:T(8,128)(2,1)} %el_ref.1), custom_call_target="tpu_custom_call" | custom-call | tf_op jit(solution)/shard_map/pallas_call | solution.py:355
  33.3 0.8 %reduce_sum.9 = f32[3,16]{1,0:T(4,128)S(1)} reduce(f32[3,16,128]{2,1,0:T(8,128)} %shard_map.64, f32[]{:T(128)} %constant.0.clone.1), dimensions={2}, to_apply=%region_0.0 | reduce | flops 6096 | bytes 24772 | tf_op jit(solution)/shard_map/reduce_sum | solution.py:384
  34.1 0.7 %reshape.3 = f32[1,1,3,2,8]{4,3,2,1,0:T(2,128)} reshape(f32[3,16]{1,0:T(4,128)S(1)} %reduce_sum.9) | data formatting | bytes 384 | tf_op jit(solution)/shard_map/reshape | solution.py:384

commit v3 on v2

--- a/solution.py
+++ b/solution.py
@@ -96,7 +96,6 @@
 
 MESH = pl.DeviceIdType.MESH
 HALF = 4
-RELAYED = (4, 5, 6, 7)
 DIRECT = (2, 3, 1)
 NT = (((1,), (1,)), ((), ()))
 NN = (((1,), (0,)), ((), ()))
@@ -194,6 +193,10 @@
         return ebuf.at[part, source * 2 + h]
 
     src_out = {}
+    depth, lane_y = s // 2, s % 2
+    inner = ((depth + 1) // 2) % 2
+    other_half = 1 - depth // 2
+    inner_at, outer_at = 1 + other_half, 3 * other_half
 
     def send_on(n, m, chunk):
         src_out[n, m] = pltpu.make_async_remote_copy(
@@ -203,9 +206,28 @@
         )
         src_out[n, m].start()
 
+    across_out = []
+    for n, there in enumerate((inner_at, outer_at)):
+        for y_flip in (0, 1):
+            peer = there * 2 + flipped(lane_y, y_flip)
+            across_out.append(
+                pltpu.make_async_remote_copy(
+                    src_ref=sendbuf.at[peer], dst_ref=slot(x, s),
+                    send_sem=src_send.at[0, HALF + 2 * n + y_flip],
+                    recv_sem=src_recv.at[0, HALF + 2 * (1 - inner) + y_flip],
+                    device_id=(peer, c), device_id_type=MESH,
+                )
+            )
+
     table_in[0].wait()
     pick_rows(0, hot, sendbuf)
-    for m in RELAYED + DIRECT:
+
+    @pl.when(inner == 1)
+    def _():
+        for copy in across_out:
+            copy.start()
+
+    for m in DIRECT:
         send_on(0, m, sendbuf.at[flipped(s, m)])
     own = [pltpu.make_async_copy(sendbuf.at[s], slot(x, s), own_sem.at[0])]
     own[0].start()
@@ -216,92 +238,149 @@
     own.append(pltpu.make_async_copy(sendother.at[s - base], slot(1 - x, s), own_sem.at[1]))
     own[1].start()
 
+    @pl.when(inner == 0)
+    def _():
+        for copy in across_out:
+            copy.start()
+
     near, across = flipped(c, 1), flipped(c, 2)
     near_out, far_out = {}, {}
 
-    def to_near(n, m):
-        chunk = slot((x, 1 - x)[n], flipped(s, m))
+    def to_near(n, m, source):
+        chunk = slot((x, 1 - x)[n], source)
         near_out[n, m] = pltpu.make_async_remote_copy(
             src_ref=chunk, dst_ref=chunk, send_sem=near_send.at[n, m], recv_sem=near_recv.at[n, m],
             device_id=(s, near), device_id_type=MESH,
         )
         near_out[n, m].start()
 
+    def relayed_from(q):
+        return (inner_at, outer_at)[q // 2] * 2 + flipped(lane_y, q % 2)
+
+    def relay(q):
+        chunk = slot(x, relayed_from(q))
+        far_out[q] = pltpu.make_async_remote_copy(
+            src_ref=chunk, dst_ref=chunk, send_sem=far_send.at[q], recv_sem=far_recv.at[q],
+            device_id=(s, across), device_id_type=MESH,
+        )
+        pltpu.make_async_remote_copy(
+            src_ref=chunk, dst_ref=chunk, send_sem=far_send.at[q], recv_sem=src_recv.at[0, HALF + q],
+            device_id=(s, across), device_id_type=MESH,
+        ).wait_recv()
+        far_out[q].start()
+        to_near(0, HALF + q, relayed_from(q))
+
     for n in (0, 1):
         own[n].wait()
-        to_near(n, 0)
-    for n in (0, 1):
-        src_out[n, 1].wait_recv()
-        to_near(n, 1)
-    for m in RELAYED:
+        to_near(n, 0, s)
+    for m in (1, 2):
         src_out[0, m].wait_recv()
-        chunk = slot(x, flipped(s, m))
-        far_out[m] = pltpu.make_async_remote_copy(
-            src_ref=chunk, dst_ref=chunk, send_sem=far_send.at[m], recv_sem=far_recv.at[m],
-            device_id=(s, across), device_id_type=MESH,
-        )
-        far_out[m].start()
-        to_near(0, m)
-    for m in (2, 3):
-        for n in (0, 1):
-            src_out[n, m].wait_recv()
-            to_near(n, m)
-    for m in RELAYED:
-        far_out[m].wait_recv()
-        to_near(1, m)
+        to_near(0, m, flipped(s, m))
+    relay(0)
+    src_out[0, 3].wait_recv()
+    to_near(0, 3, flipped(s, 3))
+    relay(1)
+    for m in (1, 2, 3):
+        src_out[1, m].wait_recv()
+        to_near(1, m, flipped(s, m))
 
     tau_in.wait()
     for copy in tau_out:
         copy.wait_recv()
     for t in range(per):
         xneg[t] = -xbuf[1, t].reshape(nv, nv)
-    for copy in near_out.values():
-        copy.wait_recv()
-
-    def nodes(k, carry):
-        left_re = ebuf[0, :, k].reshape(nv, nv)
-        left_im = ebuf[1, :, k].reshape(nv, nv)
-        right_re = ebuf[0, :, NSN + k].reshape(nv, nv)
-        right_im = ebuf[1, :, NSN + k].reshape(nv, nv)
-        for t in range(per):
-            x_re = xbuf[0, t].reshape(nv, nv)
-            x_im = xbuf[1, t].reshape(nv, nv)
-            x_neg = xneg[t]
-
-            def mm(a, b, dims):
-                return lax.dot_general(a, b, dims, preferred_element_type=f32)
-
-            def rounded(value):
-                return value.astype(bf16).astype(f32)
-
-            lt[k, t, 0] = rounded(mm(x_re, left_re, NT) + mm(x_neg, left_im, NT))
-            lt[k, t, 1] = rounded(mm(x_re, left_im, NT) + mm(x_im, left_re, NT))
-            rt[k, t, 0] = rounded(mm(right_re, x_re, NN) + mm(right_im, x_im, NN))
-            rt[k, t, 1] = rounded(mm(right_im, x_re, NN) + mm(right_re, x_neg, NN))
-        return carry
-
-    lax.fori_loop(0, NSN, nodes, 0)
+    for n in (0, 1):
+        for m in range(HALF):
+            near_out[n, m].wait_recv()
+
+    part_rows = nv // 2
+    blocks = part_rows // rows
+
+    def mm(a, b, dims):
+        return lax.dot_general(a, b, dims, preferred_element_type=f32)
+
+    def rounded(value):
+        return value.astype(bf16).astype(f32)
+
+    def nodes(side):
+        at = pl.ds(side * blocks, blocks)
+
+        def stacked(part, first, count):
+            return jnp.concatenate(
+                [ebuf[part, at, first + k].reshape(part_rows, nv) for k in range(count)], axis=0
+            )
+
+        def left_pair(j, carry):
+            left_re, left_im = stacked(0, 2 * j, 2), stacked(1, 2 * j, 2)
+            for t in range(per):
+                x_re, x_im = xbuf[0, t].reshape(nv, nv), xbuf[1, t].reshape(nv, nv)
+                re = rounded(mm(x_re, left_re, NT) + mm(xneg[t], left_im, NT))
+                im = rounded(mm(x_re, left_im, NT) + mm(x_im, left_re, NT))
+                for k in range(2):
+                    lanes = slice(k * part_rows, (k + 1) * part_rows)
+                    lt[2 * j + k, t, 0, side] = re[:, lanes]
+                    lt[2 * j + k, t, 1, side] = im[:, lanes]
+            return carry
+
+        lax.fori_loop(0, NSN // 2, left_pair, 0)
+
+        def right_time(t, carry):
+            x_re, x_im, x_neg = xbuf[0, t].reshape(nv, nv), xbuf[1, t].reshape(nv, nv), xneg[t]
+            for j in range((n_ids - NSN) // 2):
+                right_re, right_im = stacked(0, NSN + 2 * j, 2), stacked(1, NSN + 2 * j, 2)
+                re = rounded(mm(right_re, x_re, NN) + mm(right_im, x_im, NN))
+                im = rounded(mm(right_im, x_re, NN) + mm(right_re, x_neg, NN))
+                for k in range(2):
+                    down = slice(k * part_rows, (k + 1) * part_rows)
+                    for half in range(2):
+                        lanes = slice(half * part_rows, (half + 1) * part_rows)
+                        rt[2 * j + k, t, 0, side, half] = re[down, lanes]
+                        rt[2 * j + k, t, 1, side, half] = im[down, lanes]
+            return carry
+
+        lax.fori_loop(0, per, right_time, 0)
 
     n_diag = diag_ref.shape[2]
     for copy in smalls[1:]:
         copy.wait()
     picks = [(diag_ref[0, 0, d], diag_ref[1, 0, d], phase_ref[diag_ref[2, 0, d]]) for d in range(n_diag)]
-    for t in range(per):
-
+
+    def products(t, down, acrosses, sums):
         def rows_of(block, sums):
             at = pl.ds(pl.multiple_of(block * 8, 8), 8)
+            left_at = pl.ds(pl.multiple_of(down * part_rows + block * 8, 8), 8)
             sums = list(sums)
-            for half in range(nv // 128):
-                lanes = slice(half * 128, (half + 1) * 128)
+            for half in acrosses:
                 for d, (k1, k2, _) in enumerate(picks):
-                    a_re, a_im = lt[k1, t, 0, at, lanes], lt[k1, t, 1, at, lanes]
-                    b_re, b_im = rt[k2, t, 0, at, lanes], rt[k2, t, 1, at, lanes]
+                    a_re, a_im = lt[k1, t, 0, half, left_at, :], lt[k1, t, 1, half, left_at, :]
+                    b_re, b_im = rt[k2, t, 0, down, half, at, :], rt[k2, t, 1, down, half, at, :]
                     sums[2 * d] = sums[2 * d] + a_re * b_re - a_im * b_im
                     sums[2 * d + 1] = sums[2 * d + 1] + a_re * b_im + a_im * b_re
             return tuple(sums)
 
-        zero = jnp.zeros((8, 128), f32)
-        sums = lax.fori_loop(0, nv // 8, rows_of, (zero,) * (2 * n_diag))
+        return lax.fori_loop(0, part_rows // 8, rows_of, sums)
+
+    zero = jnp.zeros((8, 128), f32)
+    here, there = depth // 2, other_half
+    def pass_on(q):
+        far_out[q].wait_recv()
+        to_near(1, HALF + q, relayed_from(q))
+
+    relay(2)
+    pass_on(0)
+    nodes(here)
+    relay(3)
+    pass_on(1)
+    pass_on(2)
+    early = [products(t, here, (here,), (zero,) * (2 * n_diag)) for t in range(per)]
+    pass_on(3)
+    for n in (0, 1):
+        for q in range(4):
+            near_out[n, HALF + q].wait_recv()
+    nodes(there)
+    for t in range(per):
+        sums = products(t, here, (there,), early[t])
+        sums = products(t, there, (here, there), sums)
         real, imag = [], []
         for d, (_, _, turn) in enumerate(picks):
             cosine = (turn == 0).astype(f32) - (turn == 2).astype(f32)
@@ -334,7 +413,7 @@
         keep = (place < size).astype(f32)
         out_ref[place] = vbuf[at] * keep
 
-    for copy in list(src_out.values()) + list(far_out.values()) + list(near_out.values()):
+    for copy in list(src_out.values()) + across_out + list(far_out.values()) + list(near_out.values()):
         copy.wait_send()
     for copy in tau_out + val_out:
         copy.wait_send()
@@ -369,8 +448,8 @@
             pltpu.VMEM((2, 2 * n_src, n_ids, rows, nv), bf16),
             pltpu.VMEM((2, per, n_snk, cols, nv), bf16),
             pltpu.VMEM((per, nv, nv), bf16),
-            pltpu.VMEM((NSN, per, 2, nv, nv), f32),
-            pltpu.VMEM((n_ids - NSN, per, 2, nv, nv), f32),
+            pltpu.VMEM((NSN, per, 2, 2, nv, nv // 2), f32),
+            pltpu.VMEM((n_ids - NSN, per, 2, 2, 2, nv // 2, nv // 2), f32),
             pltpu.VMEM((sinks, 2 * n_diag, 128), f32),
             sem((4,)), sem((2,)), sem((2,)), sem, sem((4,)), sem((4,)),
         ]
@@ -390,7 +469,7 @@
         and lax.axis_size("src") == 8
         and elementals.shape[0] == 32
         and tau_cols.shape[3] % 16 == 0
-        and tau_cols.shape[4] % 128 == 0
+        and tau_cols.shape[4] == 256
     )
     return (fused_local if fits else plain_local)(tau_cols, elementals, *rest)
 

time: 35 us -> 34.5 us (0.986)
  Pallas kernels: 33.3 us -> 32.9 us
    pallas_call x1, Pallas kernels: 33.3 us -> 32.9 us  [fused_local(): pl.pallas_call(kernel, out_shape=jax.ShapeDtypeStruct((MAXB, 2 * n_diag,...]
where the time goes in v3:
time: 34.5 us; the launch traced here: 34.4 us
  Pallas kernels  32.9 us (95%)
  other arithmetic  0.82 us (2%)
  local copies, waits for them, and re-layouts  0.66 us (2%)
    pallas_call x1, Pallas kernels, fused_local(): pl.pallas_call(kernel, out_shape=jax.ShapeDtypeStruct((MAXB, 2 * n_diag,...  32.9 us
    reduce_sum x1, other arithmetic, fused_local(): return jnp.sum(partial, axis=2).reshape(1, 1, MAXB, 2, n_diag)  0.82 us

profile of v3, /device:TPU:0, one launch (start us, length us, event | category | flops | bytes accessed | tf_op | source)
XLA Modules:
  0.0 34.4 jit_solution(4841424329619146451)
XLA Ops:
  0.0 32.9 %shard_map.64 = f32[3,16,128]{2,1,0:T(8,128)} custom-call(s32[8,8]{1,0:T(8,128)} %ids_hbm.1, s32[3,1,8]{2,1,0:T(1,128)} %bitcast.1, s32[16]{0:T(128)} %phase_hbm.1, s32[4]{0:T(128)} %size_hbm.1, bf16[2,1,8,64,256]{4,3,2,1,0:T(8,128)(2,1)} %tau_ref.1, bf16[32,2,256,256]{3,2,1,0:T(8,128)(2,1)} %el_ref.1), custom_call_target="tpu_custom_call" | custom-call | tf_op jit(solution)/shard_map/pallas_call | solution.py:434
  32.9 0.8 %reduce_sum.9 = f32[3,16]{1,0:T(4,128)S(1)} reduce(f32[3,16,128]{2,1,0:T(8,128)} %shard_map.64, f32[]{:T(128)} %constant.0.clone.1), dimensions={2}, to_apply=%region_0.0 | reduce | flops 6096 | bytes 24772 | tf_op jit(solution)/shard_map/reduce_sum | solution.py:463
  33.7 0.7 %reshape.3 = f32[1,1,3,2,8]{4,3,2,1,0:T(2,128)} reshape(f32[3,16]{1,0:T(4,128)S(1)} %reduce_sum.9) | data formatting | bytes 384 | tf_op jit(solution)/shard_map/reshape | solution.py:463
